TPU v7x, 32 devices: a whole 2x2x4 slice. The times are simulated.
32 devices in a mesh: mod: 4 (over z), frm: 2 (over x), ori: 4 (over y, core).
Axes of the slice: x: 2, y: 2, z: 4, core: 2. Of those that a mesh axis runs over, the one named last changes fastest.
Arguments:
- counts: int32 [512, 128, 128], P(('frm', 'ori'), 'mod'), may hold values from 0 to 8
- slice_codes: int32 [4096, 128, 128], P('ori', ('mod', 'frm')), may hold values from 0 to 2047
- pixel_mask: int32 [128, 128], P('mod'), may hold values 0 or 1
Outputs:
- log_posterior: float32 [2, 256, 4096], P('frm', 'mod', 'ori')
All inputs are finite; a program needn't handle non-finite values. No bound on the sum of `pixel_mask` on one device may be relied on, other than what follows from the above.
Results may differ from a plain program's by a relative error of at most 0.0024.
Values may be sent and summed in bfloat16 or wider, within the bound.
A program may use at most 64 MiB of HBM per device.

v0:
```python
import math
import jax
import jax.numpy as jnp
from jax import lax
from jax.sharding import PartitionSpec as P

PASSES = 8
TIME_STEP = 0.2
EDGE_SCALE = 2.0
LOG_FLOOR = -7.0
CODE_STEP = 1.0 / 256.0


def extended(x, sides, width):
    for axis, dim in sides:
        peers, length = (lax.axis_size(axis), x.shape[dim])
        up = [(i, (i + 1) % peers) for i in range(peers - 1)]
        down = [(j, i) for i, j in up]
        last = lax.slice_in_dim(x, length - width, length, axis=dim)
        leading = lax.slice_in_dim(x, 0, width, axis=dim)
        before = lax.ppermute(last, axis, up)
        after = lax.ppermute(leading, axis, down)
        x = jnp.concatenate([before, x, after], axis=dim)
    return x


def conduct(difference):
    ratio = difference / EDGE_SCALE
    return difference / (1.0 + ratio * ratio)


def relax_once(padded):
    centre = padded[:, 1:-1, :]
    column_pad = jnp.zeros((centre.shape[0], centre.shape[1], 1), jnp.float32)
    left_side = jnp.concatenate([column_pad, centre[:, :, :-1]], axis=2)
    right_side = jnp.concatenate([centre[:, :, 1:], column_pad], axis=2)
    flux_sum = conduct(padded[:, :-2, :] - centre) + conduct(padded[:, 2:, :] - centre)
    flux_sum = flux_sum + conduct(left_side - centre) + conduct(right_side - centre)
    return centre + TIME_STEP * flux_sum


def body(counts, slice_codes, pixel_mask):
    intensity = counts.astype(jnp.float32)
    module_rows = intensity.shape[1]
    total_rows = module_rows * lax.axis_size("mod")
    first_row = lax.axis_index("mod") * module_rows
    row_ids = first_row - 1 + lax.broadcasted_iota(jnp.int32, (1, module_rows + 2, 1), 1)
    inside = ((row_ids >= 0) & (row_ids < total_rows)).astype(jnp.float32)
    for pair_index in range(PASSES // 2):
        padded = extended(intensity, (("mod", 1),), 2)
        widened = relax_once(padded) * inside
        intensity = relax_once(widened)
    cleaned = intensity.astype(jnp.bfloat16) * pixel_mask.astype(jnp.bfloat16)[None]
    gathered = lax.all_gather(cleaned, "ori", axis=0, tiled=True)
    log_slices = (LOG_FLOOR + slice_codes.astype(jnp.float32) * CODE_STEP).astype(jnp.bfloat16)
    band_rows = log_slices.shape[1]
    own_mask = lax.dynamic_slice_in_dim(
        pixel_mask, lax.axis_index("frm") * band_rows, band_rows, 0
    ).astype(jnp.float32)
    local_totals = jnp.sum(jnp.exp(log_slices.astype(jnp.float32)) * own_mask[None], axis=(1, 2))
    module_totals = lax.psum(local_totals, "frm")
    product = lax.dot_general(
        gathered,
        lax.all_gather(log_slices, "frm", axis=1, tiled=True),
        (((1, 2), (1, 2)), ((), ())),
        preferred_element_type=jnp.float32,
    )
    partial_value = product - module_totals[None, :]
    scale_factor = 1.0 / math.sqrt(module_rows * lax.axis_size("mod") * intensity.shape[2])
    summed = lax.psum(partial_value, "mod")
    share_rows = summed.shape[0] // lax.axis_size("mod")
    own_rows = lax.dynamic_slice_in_dim(summed, lax.axis_index("mod") * share_rows, share_rows, 0)
    scores = own_rows * scale_factor
    peaks = lax.pmax(jnp.max(scores, axis=1), "ori")
    masses = lax.psum(jnp.sum(jnp.exp(scores - peaks[:, None]), axis=1), "ori")
    log_posterior = scores - (peaks + jnp.log(masses))[:, None]
    return log_posterior[None]


def solution(mesh):
    in_specs = (P(("frm", "ori"), "mod", None), P("ori", ("mod", "frm"), None), P("mod", None))
    out_specs = P("frm", "mod", "ori")
    return jax.shard_map(body, mesh=mesh, in_specs=in_specs, out_specs=out_specs, check_vma=False)
```

profile of v0, /device:TPU:0, one launch (start us, length us, event | category | flops | bytes accessed | tf_op | source)
XLA Modules:
  0.0 270.0 jit_solution(14299693022543329256)
XLA Ops:
  6.5 1.8 copy_convert_fusion.1
  8.4 5.0 %collective-permute-start = (f32[64,2,128]{2,0,1:T(8,128)S(1)}, f32[64,2,128]{2,0,1:T(8,128)S(1)}, u32[]{:S(2)}, u32[]{:S(2)}) collective-permute-start(f32[64,2,128]{2,0,1:T(8,128)S(1)} %get-tuple-element.29), channel_id=1, source_target_pairs={{0,8},{8,16},{16,24},{1,9},{9,17},{17,25},{2,10},{10,18},{18,26},{... | collective-permute-start | bytes 196616 | tf_op jit(solution)/shard_map/ppermute | solution.py:21
  13.4 1.3 collective-permute-start.1
  15.2 4.3 %collective-permute-done.1 = f32[64,2,128]{2,0,1:T(8,128)S(1)} collective-permute-done((f32[64,2,128]{2,0,1:T(8,128)S(1)}, f32[64,2,128]{2,0,1:T(8,128)S(1)}, u32[]{:S(2)}, u32[]{:S(2)}) %collective-permute-start.1) | collective-permute-done | bytes 65568 | tf_op jit(solution)/shard_map/ppermute | solution.py:22
  22.7 3.5 %collective-permute-start.2 = (f32[64,2,128]{2,0,1:T(8,128)S(1)}, f32[64,2,128]{2,0,1:T(8,128)S(1)}, u32[]{:S(2)}, u32[]{:S(2)}) collective-permute-start(f32[64,2,128]{2,0,1:T(8,128)S(1)} %get-tuple-element.27), channel_id=1, source_target_pairs={{0,8},{8,16},{16,24},{1,9},{9,17},{17,25},{2,10},{10,18},{18,26},{... | collective-permute-start | bytes 196616 | tf_op jit(solution)/shard_map/ppermute | solution.py:21
  26.2 1.3 collective-permute-start.3
  28.1 4.3 %collective-permute-done.3 = f32[64,2,128]{2,0,1:T(8,128)S(1)} collective-permute-done((f32[64,2,128]{2,0,1:T(8,128)S(1)}, f32[64,2,128]{2,0,1:T(8,128)S(1)}, u32[]{:S(2)}, u32[]{:S(2)}) %collective-permute-start.3) | collective-permute-done | bytes 65568 | tf_op jit(solution)/shard_map/ppermute | solution.py:22
  32.9 1.2 add_multiply_fusion.2
  35.6 3.5 %collective-permute-start.4 = (f32[64,2,128]{2,0,1:T(8,128)S(1)}, f32[64,2,128]{2,0,1:T(8,128)S(1)}, u32[]{:S(2)}, u32[]{:S(2)}) collective-permute-start(f32[64,2,128]{2,0,1:T(8,128)S(1)} %get-tuple-element.25), channel_id=1, source_target_pairs={{0,8},{8,16},{16,24},{1,9},{9,17},{17,25},{2,10},{10,18},{18,26},{... | collective-permute-start | bytes 196616 | tf_op jit(solution)/shard_map/ppermute | solution.py:21
  39.1 1.3 collective-permute-start.5
  41.0 4.3 %collective-permute-done.5 = f32[64,2,128]{2,0,1:T(8,128)S(1)} collective-permute-done((f32[64,2,128]{2,0,1:T(8,128)S(1)}, f32[64,2,128]{2,0,1:T(8,128)S(1)}, u32[]{:S(2)}, u32[]{:S(2)}) %collective-permute-start.5) | collective-permute-done | bytes 65568 | tf_op jit(solution)/shard_map/ppermute | solution.py:22
  48.6 1.9 collective-permute-start.6
  50.5 1.5 collective-permute-start.7
  52.4 4.3 %collective-permute-done.7 = f32[64,2,128]{2,0,1:T(8,128)S(1)} collective-permute-done((f32[64,2,128]{2,0,1:T(8,128)S(1)}, f32[64,2,128]{2,0,1:T(8,128)S(1)}, u32[]{:S(2)}, u32[]{:S(2)}) %collective-permute-start.7) | collective-permute-done | bytes 65568 | tf_op jit(solution)/shard_map/ppermute | solution.py:22
  58.7 2.0 fusion.4
  60.8 7.8 %multiply_reduce_fusion = (f32[1024]{0:T(1024)S(1)}, bf16[1024,16,128]{2,0,1:T(8,128)(2,1)}) fusion(f32[16,128]{1,0:T(8,128)S(1)} %dynamic-slice_convert_fusion, s32[1024,16,128]{2,1,0:T(8,128)} %param.4), kind=kLoop, calls=%fused_computation.4 | loop fusion | flops 14679040 | bytes 12595200 | tf_op jit(solution)/shard_map/reduce_sum | solution.py:60
  68.6 4.9 %psum.21 = f32[1024]{0:T(1024)S(1)} all-reduce(f32[1024]{0:T(1024)S(1)} %get-tuple-element.5), channel_id=1, replica_groups=mesh['mod'=4,'frm'=2,'ori'=4] {'frm'}, use_global_device_ids=true, to_apply=%region_1.0 | all-reduce | flops 1024 | bytes 8192 | tf_op jit(solution)/shard_map/psum | solution.py:61
  73.6 8.1 %all-gather.3.cloned.1.call-done = bf16[256,32,128]{2,0,1:T(8,128)(2,1)} async-done(((bf16[64,32,128]{2,0,1:T(8,128)(2,1)}), bf16[256,32,128]{2,0,1:T(8,128)(2,1)}) %all-gather.3.cloned.1.call-update) | async-done | bytes 2097168 | tf_op jit(solution)/shard_map/all_gather | solution.py:54
  81.7 105.5 %all-gather.5.cloned.1.call-done = bf16[1024,32,128]{2,0,1:T(8,128)(2,1)} async-done(((bf16[1024,16,128]{2,0,1:T(8,128)(2,1)}), bf16[1024,32,128]{2,0,1:T(8,128)(2,1)}) %all-gather.5.cloned.1.call-update) | async-done | bytes 8388624 | tf_op jit(solution)/shard_map/all_gather | solution.py:64
  187.2 7.4 %fusion.3 = f32[256,1024]{1,0:T(8,128)} fusion(bf16[256,32,128]{2,0,1:T(8,128)(2,1)} %all-gather.3.cloned.1.call-done, bf16[1024,32,128]{2,0,1:T(8,128)(2,1)} %all-gather.5.cloned.1.call-done, f32[1024]{0:T(1024)S(1)} %psum.21), kind=kOutput, calls=%fused_computation.6 | convolution fusion | flops 2147745792 | bytes 11538432 | tf_op jit(solution)/shard_map/dot_general | solution.py:62
  194.7 52.1 %all-reduce.18.cloned.1.call-done = f32[256,1024]{1,0:T(8,128)} async-done(((f32[256,1024]{1,0:T(8,128)}), f32[256,1024]{1,0:T(8,128)}) %all-reduce.18.cloned.1.call-update) | async-done | bytes 1048592 | tf_op jit(solution)/shard_map/psum | solution.py:70
  247.8 6.9 %pmax.7 = f32[64]{0:T(128)S(1)} all-reduce(f32[64]{0:T(128)S(1)} %fusion.5), channel_id=1, replica_groups=mesh['mod'=4,'frm'=2,'ori'=4] {'ori'}, use_global_device_ids=true, to_apply=%region_4.0 | all-reduce | flops 64 | bytes 512 | tf_op jit(solution)/shard_map/pmax | solution.py:74
  255.8 5.9 %psum.23 = f32[64]{0:T(128)S(1)} all-reduce(f32[64]{0:T(128)S(1)} %exponential_reduce_fusion), channel_id=1, replica_groups=mesh['mod'=4,'frm'=2,'ori'=4] {'ori'}, use_global_device_ids=true, to_apply=%region_6.0 | all-reduce | flops 64 | bytes 512 | tf_op jit(solution)/shard_map/psum | solution.py:75
  261.8 1.7 subtract_bitcast_fusion
  (40 shorter events, 15.0 us)
Async XLA Ops:
  6.5 75.1 %all-gather.3.cloned.1.call-start = ((), (), s32[]{:S(2)}) async-start(), calls=%async_computation | async-start | bytes 2621440 | tf_op jit(solution)/shard_map/all_gather | solution.py:54
  8.4 6.9 %collective-permute-start = (f32[64,2,128]{2,0,1:T(8,128)S(1)}, f32[64,2,128]{2,0,1:T(8,128)S(1)}, u32[]{:S(2)}, u32[]{:S(2)}) collective-permute-start(f32[64,2,128]{2,0,1:T(8,128)S(1)} %get-tuple-element.29), channel_id=1, source_target_pairs={{0,8},{8,16},{16,24},{1,9},{9,17},{17,25},{2,10},{10,18},{18,26},{... | collective-permute-start | bytes 196616 | tf_op jit(solution)/shard_map/ppermute | solution.py:21
  13.4 6.2 %collective-permute-start.1 = (f32[64,2,128]{2,0,1:T(8,128)S(1)}, f32[64,2,128]{2,0,1:T(8,128)S(1)}, u32[]{:S(2)}, u32[]{:S(2)}) collective-permute-start(f32[64,2,128]{2,0,1:T(8,128)S(1)} %get-tuple-element.30), channel_id=1, source_target_pairs={{8,0},{16,8},{24,16},{9,1},{17,9},{25,17},{10,2},{18,10},{26,18},{... | collective-permute-start | bytes 196616 | tf_op jit(solution)/shard_map/ppermute | solution.py:22
  22.7 5.4 %collective-permute-start.2 = (f32[64,2,128]{2,0,1:T(8,128)S(1)}, f32[64,2,128]{2,0,1:T(8,128)S(1)}, u32[]{:S(2)}, u32[]{:S(2)}) collective-permute-start(f32[64,2,128]{2,0,1:T(8,128)S(1)} %get-tuple-element.27), channel_id=1, source_target_pairs={{0,8},{8,16},{16,24},{1,9},{9,17},{17,25},{2,10},{10,18},{18,26},{... | collective-permute-start | bytes 196616 | tf_op jit(solution)/shard_map/ppermute | solution.py:21
  26.2 6.2 %collective-permute-start.3 = (f32[64,2,128]{2,0,1:T(8,128)S(1)}, f32[64,2,128]{2,0,1:T(8,128)S(1)}, u32[]{:S(2)}, u32[]{:S(2)}) collective-permute-start(f32[64,2,128]{2,0,1:T(8,128)S(1)} %get-tuple-element.28), channel_id=1, source_target_pairs={{8,0},{16,8},{24,16},{9,1},{17,9},{25,17},{10,2},{18,10},{26,18},{... | collective-permute-start | bytes 196616 | tf_op jit(solution)/shard_map/ppermute | solution.py:22
  35.6 5.4 %collective-permute-start.4 = (f32[64,2,128]{2,0,1:T(8,128)S(1)}, f32[64,2,128]{2,0,1:T(8,128)S(1)}, u32[]{:S(2)}, u32[]{:S(2)}) collective-permute-start(f32[64,2,128]{2,0,1:T(8,128)S(1)} %get-tuple-element.25), channel_id=1, source_target_pairs={{0,8},{8,16},{16,24},{1,9},{9,17},{17,25},{2,10},{10,18},{18,26},{... | collective-permute-start | bytes 196616 | tf_op jit(solution)/shard_map/ppermute | solution.py:21
  39.1 6.2 %collective-permute-start.5 = (f32[64,2,128]{2,0,1:T(8,128)S(1)}, f32[64,2,128]{2,0,1:T(8,128)S(1)}, u32[]{:S(2)}, u32[]{:S(2)}) collective-permute-start(f32[64,2,128]{2,0,1:T(8,128)S(1)} %get-tuple-element.26), channel_id=1, source_target_pairs={{8,0},{16,8},{24,16},{9,1},{17,9},{25,17},{10,2},{18,10},{26,18},{... | collective-permute-start | bytes 196616 | tf_op jit(solution)/shard_map/ppermute | solution.py:22
  47.4 4.5 %copy-start = (s32[32,128]{1,0:T(8,128)S(1)}, s32[32,128]{1,0:T(8,128)}, u32[]{:S(2)}) copy-start(s32[32,128]{1,0:T(8,128)} %param.5) | copy-start | bytes 49156
  48.6 3.8 %collective-permute-start.6 = (f32[64,2,128]{2,0,1:T(8,128)S(1)}, f32[64,2,128]{2,0,1:T(8,128)S(1)}, u32[]{:S(2)}, u32[]{:S(2)}) collective-permute-start(f32[64,2,128]{2,0,1:T(8,128)S(1)} %get-tuple-element.23), channel_id=1, source_target_pairs={{0,8},{8,16},{16,24},{1,9},{9,17},{17,25},{2,10},{10,18},{18,26},{... | collective-permute-start | bytes 196616 | tf_op jit(solution)/shard_map/ppermute | solution.py:21
  50.5 6.2 %collective-permute-start.7 = (f32[64,2,128]{2,0,1:T(8,128)S(1)}, f32[64,2,128]{2,0,1:T(8,128)S(1)}, u32[]{:S(2)}, u32[]{:S(2)}) collective-permute-start(f32[64,2,128]{2,0,1:T(8,128)S(1)} %get-tuple-element.24), channel_id=1, source_target_pairs={{8,0},{16,8},{24,16},{9,1},{17,9},{25,17},{10,2},{18,10},{26,18},{... | collective-permute-start | bytes 196616 | tf_op jit(solution)/shard_map/ppermute | solution.py:22
  60.7 126.5 %all-gather.5.cloned.1.call-start = ((), (), s32[]{:S(2)}) async-start(), calls=%async_computation.1 | async-start | bytes 12582912 | tf_op jit(solution)/shard_map/all_gather | solution.py:64
  68.6 178.1 %all-reduce.18.cloned.1.call-start = ((), (), s32[]{:S(2)}) async-start(), calls=%async_computation.2 | async-start | bytes 2097152 | tf_op jit(solution)/shard_map/psum | solution.py:70
Sparse Core Ops, SparseCore 0:
  60.9 20.7 all-gather.2
  83.2 103.9 all-gather.4
  194.8 51.8 all-reduce.17
where the time goes:
time: 271 us; the launch traced here: 270 us
  waiting for transfers between devices  185 us (68%)
  other arithmetic  24.2 us (9%)
  starting transfers between devices  19.3 us (7%)
  blocking collectives  17.7 us (7%)
  between operations  13.4 us (5%)
  matrix products  7.45 us (3%)
  local copies, waits for them, and re-layouts  3.11 us (1%)
    all_gather x1, waiting for transfers between devices, body(): lax.all_gather(log_slices, 'frm', axis=1, tiled=True)  106 us
    psum x1, waiting for transfers between devices, body(): summed = lax.psum(partial_value, 'mod')  52.1 us
    ppermute x4, waiting for transfers between devices, extended(): after = lax.ppermute(leading, axis, down)  17.1 us
    ppermute x4, starting transfers between devices, extended(): before = lax.ppermute(last, axis, up)  13.8 us
    all_gather x1, waiting for transfers between devices, body(): gathered = lax.all_gather(cleaned, 'ori', axis=0, tiled=True)  8.08 us
    reduce_sum x1, other arithmetic, body(): jnp.sum(jnp.exp(log_slices.astype(jnp.float32)) * own_mask[None], axis=(1...  7.77 us
    dot_general x1, matrix products, body(): lax.dot_general(gathered, lax.all_gather(log_slices, 'frm', axis=1, tiled...  7.45 us
    pmax x1, blocking collectives, body(): peaks = lax.pmax(jnp.max(scores, axis=1), 'ori')  6.85 us
  transfers between devices with their start and end apart: 11, of which 11 were waited for; matrix products, arithmetic and copies ran while one was open for 3% of the time, Pallas kernels for 0%

commit v1 on v0

--- a/solution.py
+++ b/solution.py
@@ -67,7 +67,9 @@
     )
     partial_value = product - module_totals[None, :]
     scale_factor = 1.0 / math.sqrt(module_rows * lax.axis_size("mod") * intensity.shape[2])
-    summed = lax.psum(partial_value, "mod")
+    summed = partial_value
+    for hop in (1, 2):
+        summed = summed + lax.ppermute(summed, "mod", [(dev, dev ^ hop) for dev in range(4)])
     share_rows = summed.shape[0] // lax.axis_size("mod")
     own_rows = lax.dynamic_slice_in_dim(summed, lax.axis_index("mod") * share_rows, share_rows, 0)
     scores = own_rows * scale_factor

time: 271 us -> 286 us (1.055)
  waiting for transfers between devices: 185 us -> 201 us
  starting transfers between devices: 19.3 us -> 23.3 us
    ppermute x0 -> x2, waiting for transfers between devices: none -> 68.1 us  [body(): lax.ppermute(summed, 'mod', [(dev, dev ^ hop) for dev in range(4)])]
    psum x1 -> x0, waiting for transfers between devices: 52.1 us -> none  [body(): summed = lax.psum(partial_value, 'mod')]
    ppermute x0 -> x2, starting transfers between devices: none -> 4.02 us  [body(): lax.ppermute(summed, 'mod', [(dev, dev ^ hop) for dev in range(4)])]
  transfers between devices with their start and end apart: 11 -> 12, of which waited for: 11 -> 12; matrix products, arithmetic and copies ran while one was open for 3% -> 3% of each run, Pallas kernels for 0% -> 0%
where the time goes in v1:
time: 286 us
  waiting for transfers between devices  201 us (70%)
  starting transfers between devices  23.3 us (8%)
  other arithmetic  21.4 us (7%)
  blocking collectives  17.2 us (6%)
  between operations  13.7 us (5%)
  matrix products  6.37 us (2%)
  local copies, waits for them, and re-layouts  3.1 us (1%)
    all_gather x1, waiting for transfers between devices, body(): lax.all_gather(log_slices, 'frm', axis=1, tiled=True)  106 us
    ppermute x2, waiting for transfers between devices, body(): lax.ppermute(summed, 'mod', [(dev, dev ^ hop) for dev in range(4)])  68.1 us
    ppermute x4, waiting for transfers between devices, extended(): after = lax.ppermute(leading, axis, down)  17.1 us
    ppermute x4, starting transfers between devices, extended(): before = lax.ppermute(last, axis, up)  13.8 us
    all_gather x1, waiting for transfers between devices, body(): gathered = lax.all_gather(cleaned, 'ori', axis=0, tiled=True)  8.13 us
    reduce_sum x1, other arithmetic, body(): jnp.sum(jnp.exp(log_slices.astype(jnp.float32)) * own_mask[None], axis=(1...  7.77 us
    psum x1, blocking collectives, body(): masses = lax.psum(jnp.sum(jnp.exp(scores - peaks[:, None]), axis=1), 'ori')  6.44 us
    dot_general x1, matrix products, body(): lax.dot_general(gathered, lax.all_gather(log_slices, 'frm', axis=1, tiled...  6.37 us
  transfers between devices with their start and end apart: 12, of which 12 were waited for; matrix products, arithmetic and copies ran while one was open for 3% of the time, Pallas kernels for 0%

profile of v1, /device:TPU:0, one launch (start us, length us, event | category | flops | bytes accessed | tf_op | source)
XLA Modules:
  0.0 286.1 jit_solution(6544440310067976598)
XLA Ops:
  6.5 1.8 copy_convert_fusion.1
  8.4 5.0 %collective-permute-start = (f32[64,2,128]{2,0,1:T(8,128)S(1)}, f32[64,2,128]{2,0,1:T(8,128)S(1)}, u32[]{:S(2)}, u32[]{:S(2)}) collective-permute-start(f32[64,2,128]{2,0,1:T(8,128)S(1)} %get-tuple-element.31), channel_id=1, source_target_pairs={{0,8},{8,16},{16,24},{1,9},{9,17},{17,25},{2,10},{10,18},{18,26},{... | collective-permute-start | bytes 196616 | tf_op jit(solution)/shard_map/ppermute | solution.py:21
  13.4 1.3 collective-permute-start.1
  15.2 4.3 %collective-permute-done.1 = f32[64,2,128]{2,0,1:T(8,128)S(1)} collective-permute-done((f32[64,2,128]{2,0,1:T(8,128)S(1)}, f32[64,2,128]{2,0,1:T(8,128)S(1)}, u32[]{:S(2)}, u32[]{:S(2)}) %collective-permute-start.1) | collective-permute-done | bytes 65568 | tf_op jit(solution)/shard_map/ppermute | solution.py:22
  22.7 3.5 %collective-permute-start.2 = (f32[64,2,128]{2,0,1:T(8,128)S(1)}, f32[64,2,128]{2,0,1:T(8,128)S(1)}, u32[]{:S(2)}, u32[]{:S(2)}) collective-permute-start(f32[64,2,128]{2,0,1:T(8,128)S(1)} %get-tuple-element.29), channel_id=1, source_target_pairs={{0,8},{8,16},{16,24},{1,9},{9,17},{17,25},{2,10},{10,18},{18,26},{... | collective-permute-start | bytes 196616 | tf_op jit(solution)/shard_map/ppermute | solution.py:21
  26.2 1.3 collective-permute-start.3
  28.1 4.3 %collective-permute-done.3 = f32[64,2,128]{2,0,1:T(8,128)S(1)} collective-permute-done((f32[64,2,128]{2,0,1:T(8,128)S(1)}, f32[64,2,128]{2,0,1:T(8,128)S(1)}, u32[]{:S(2)}, u32[]{:S(2)}) %collective-permute-start.3) | collective-permute-done | bytes 65568 | tf_op jit(solution)/shard_map/ppermute | solution.py:22
  35.6 3.5 %collective-permute-start.4 = (f32[64,2,128]{2,0,1:T(8,128)S(1)}, f32[64,2,128]{2,0,1:T(8,128)S(1)}, u32[]{:S(2)}, u32[]{:S(2)}) collective-permute-start(f32[64,2,128]{2,0,1:T(8,128)S(1)} %get-tuple-element.27), channel_id=1, source_target_pairs={{0,8},{8,16},{16,24},{1,9},{9,17},{17,25},{2,10},{10,18},{18,26},{... | collective-permute-start | bytes 196616 | tf_op jit(solution)/shard_map/ppermute | solution.py:21
  41.0 4.3 %collective-permute-done.5 = f32[64,2,128]{2,0,1:T(8,128)S(1)} collective-permute-done((f32[64,2,128]{2,0,1:T(8,128)S(1)}, f32[64,2,128]{2,0,1:T(8,128)S(1)}, u32[]{:S(2)}, u32[]{:S(2)}) %collective-permute-start.5) | collective-permute-done | bytes 65568 | tf_op jit(solution)/shard_map/ppermute | solution.py:22
  48.6 1.9 collective-permute-start.6
  50.5 1.5 collective-permute-start.7
  52.4 4.3 %collective-permute-done.7 = f32[64,2,128]{2,0,1:T(8,128)S(1)} collective-permute-done((f32[64,2,128]{2,0,1:T(8,128)S(1)}, f32[64,2,128]{2,0,1:T(8,128)S(1)}, u32[]{:S(2)}, u32[]{:S(2)}) %collective-permute-start.7) | collective-permute-done | bytes 65568 | tf_op jit(solution)/shard_map/ppermute | solution.py:22
  58.7 2.0 fusion.4
  60.8 7.8 %multiply_reduce_fusion = (f32[1024]{0:T(1024)S(1)}, bf16[1024,16,128]{2,0,1:T(8,128)(2,1)}) fusion(f32[16,128]{1,0:T(8,128)S(1)} %dynamic-slice_convert_fusion, s32[1024,16,128]{2,1,0:T(8,128)} %param.4), kind=kLoop, calls=%fused_computation.4 | loop fusion | flops 14679040 | bytes 12595200 | tf_op jit(solution)/shard_map/reduce_sum | solution.py:60
  68.6 4.9 %psum.14 = f32[1024]{0:T(1024)S(1)} all-reduce(f32[1024]{0:T(1024)S(1)} %get-tuple-element.7), channel_id=1, replica_groups=mesh['mod'=4,'frm'=2,'ori'=4] {'frm'}, use_global_device_ids=true, to_apply=%region_1.0 | all-reduce | flops 1024 | bytes 8192 | tf_op jit(solution)/shard_map/psum | solution.py:61
  73.5 8.1 %all-gather.3.cloned.1.call-done = bf16[256,32,128]{2,0,1:T(8,128)(2,1)} async-done(((bf16[64,32,128]{2,0,1:T(8,128)(2,1)}), bf16[256,32,128]{2,0,1:T(8,128)(2,1)}) %all-gather.3.cloned.1.call-update) | async-done | bytes 2097168 | tf_op jit(solution)/shard_map/all_gather | solution.py:54
  81.7 105.5 %all-gather.5.cloned.1.call-done = bf16[1024,32,128]{2,0,1:T(8,128)(2,1)} async-done(((bf16[1024,16,128]{2,0,1:T(8,128)(2,1)}), bf16[1024,32,128]{2,0,1:T(8,128)(2,1)}) %all-gather.5.cloned.1.call-update) | async-done | bytes 8388624 | tf_op jit(solution)/shard_map/all_gather | solution.py:64
  187.2 6.4 %fusion.3 = f32[256,1024]{1,0:T(8,128)S(1)} fusion(bf16[256,32,128]{2,0,1:T(8,128)(2,1)} %all-gather.3.cloned.1.call-done, bf16[1024,32,128]{2,0,1:T(8,128)(2,1)} %all-gather.5.cloned.1.call-done, f32[1024]{0:T(1024)S(1)} %psum.14), kind=kOutput, calls=%fused_computation.6 | convolution fusion | flops 2147745792 | bytes 11538432 | tf_op jit(solution)/shard_map/dot_general | solution.py:62
  193.6 1.6 collective-permute-start.8
  195.1 23.2 %collective-permute-done.8 = f32[256,1024]{1,0:T(8,128)S(1)} collective-permute-done((f32[256,1024]{1,0:T(8,128)S(1)}, f32[256,1024]{1,0:T(8,128)S(1)}, u32[]{:S(2)}, u32[]{:S(2)}) %collective-permute-start.8) | collective-permute-done | bytes 1048608 | tf_op jit(solution)/shard_map/ppermute | solution.py:72
  218.5 2.5 collective-permute-start.9
  221.0 44.8 %collective-permute-done.9 = f32[256,1024]{1,0:T(8,128)S(1)} collective-permute-done((f32[256,1024]{1,0:T(8,128)S(1)}, f32[256,1024]{1,0:T(8,128)S(1)}, u32[]{:S(2)}, u32[]{:S(2)}) %collective-permute-start.9) | collective-permute-done | bytes 1048608 | tf_op jit(solution)/shard_map/ppermute | solution.py:72
  266.0 5.8 %pmax.7 = f32[64]{0:T(128)S(1)} all-reduce(f32[64]{0:T(128)S(1)} %get-tuple-element.5), channel_id=1, replica_groups=mesh['mod'=4,'frm'=2,'ori'=4] {'ori'}, use_global_device_ids=true, to_apply=%region_3.0 | all-reduce | flops 64 | bytes 512 | tf_op jit(solution)/shard_map/pmax | solution.py:76
  272.0 6.4 %psum.15 = f32[64]{0:T(128)S(1)} all-reduce(f32[64]{0:T(128)S(1)} %exponential_reduce_fusion), channel_id=1, replica_groups=mesh['mod'=4,'frm'=2,'ori'=4] {'ori'}, use_global_device_ids=true, to_apply=%region_5.0 | all-reduce | flops 64 | bytes 512 | tf_op jit(solution)/shard_map/psum | solution.py:77
  (42 shorter events, 16.5 us)
Async XLA Ops:
  6.5 75.1 %all-gather.3.cloned.1.call-start = ((), (), s32[]{:S(2)}) async-start(), calls=%async_computation | async-start | bytes 2621440 | tf_op jit(solution)/shard_map/all_gather | solution.py:54
  8.4 6.9 %collective-permute-start = (f32[64,2,128]{2,0,1:T(8,128)S(1)}, f32[64,2,128]{2,0,1:T(8,128)S(1)}, u32[]{:S(2)}, u32[]{:S(2)}) collective-permute-start(f32[64,2,128]{2,0,1:T(8,128)S(1)} %get-tuple-element.31), channel_id=1, source_target_pairs={{0,8},{8,16},{16,24},{1,9},{9,17},{17,25},{2,10},{10,18},{18,26},{... | collective-permute-start | bytes 196616 | tf_op jit(solution)/shard_map/ppermute | solution.py:21
  13.4 6.2 %collective-permute-start.1 = (f32[64,2,128]{2,0,1:T(8,128)S(1)}, f32[64,2,128]{2,0,1:T(8,128)S(1)}, u32[]{:S(2)}, u32[]{:S(2)}) collective-permute-start(f32[64,2,128]{2,0,1:T(8,128)S(1)} %get-tuple-element.32), channel_id=1, source_target_pairs={{8,0},{16,8},{24,16},{9,1},{17,9},{25,17},{10,2},{18,10},{26,18},{... | collective-permute-start | bytes 196616 | tf_op jit(solution)/shard_map/ppermute | solution.py:22
  22.7 5.4 %collective-permute-start.2 = (f32[64,2,128]{2,0,1:T(8,128)S(1)}, f32[64,2,128]{2,0,1:T(8,128)S(1)}, u32[]{:S(2)}, u32[]{:S(2)}) collective-permute-start(f32[64,2,128]{2,0,1:T(8,128)S(1)} %get-tuple-element.29), channel_id=1, source_target_pairs={{0,8},{8,16},{16,24},{1,9},{9,17},{17,25},{2,10},{10,18},{18,26},{... | collective-permute-start | bytes 196616 | tf_op jit(solution)/shard_map/ppermute | solution.py:21
  26.2 6.2 %collective-permute-start.3 = (f32[64,2,128]{2,0,1:T(8,128)S(1)}, f32[64,2,128]{2,0,1:T(8,128)S(1)}, u32[]{:S(2)}, u32[]{:S(2)}) collective-permute-start(f32[64,2,128]{2,0,1:T(8,128)S(1)} %get-tuple-element.30), channel_id=1, source_target_pairs={{8,0},{16,8},{24,16},{9,1},{17,9},{25,17},{10,2},{18,10},{26,18},{... | collective-permute-start | bytes 196616 | tf_op jit(solution)/shard_map/ppermute | solution.py:22
  35.6 5.4 %collective-permute-start.4 = (f32[64,2,128]{2,0,1:T(8,128)S(1)}, f32[64,2,128]{2,0,1:T(8,128)S(1)}, u32[]{:S(2)}, u32[]{:S(2)}) collective-permute-start(f32[64,2,128]{2,0,1:T(8,128)S(1)} %get-tuple-element.27), channel_id=1, source_target_pairs={{0,8},{8,16},{16,24},{1,9},{9,17},{17,25},{2,10},{10,18},{18,26},{... | collective-permute-start | bytes 196616 | tf_op jit(solution)/shard_map/ppermute | solution.py:21
  39.1 6.2 %collective-permute-start.5 = (f32[64,2,128]{2,0,1:T(8,128)S(1)}, f32[64,2,128]{2,0,1:T(8,128)S(1)}, u32[]{:S(2)}, u32[]{:S(2)}) collective-permute-start(f32[64,2,128]{2,0,1:T(8,128)S(1)} %get-tuple-element.28), channel_id=1, source_target_pairs={{8,0},{16,8},{24,16},{9,1},{17,9},{25,17},{10,2},{18,10},{26,18},{... | collective-permute-start | bytes 196616 | tf_op jit(solution)/shard_map/ppermute | solution.py:22
  47.4 4.5 %copy-start = (s32[32,128]{1,0:T(8,128)S(1)}, s32[32,128]{1,0:T(8,128)}, u32[]{:S(2)}) copy-start(s32[32,128]{1,0:T(8,128)} %param.5) | copy-start | bytes 49156
  48.6 3.8 %collective-permute-start.6 = (f32[64,2,128]{2,0,1:T(8,128)S(1)}, f32[64,2,128]{2,0,1:T(8,128)S(1)}, u32[]{:S(2)}, u32[]{:S(2)}) collective-permute-start(f32[64,2,128]{2,0,1:T(8,128)S(1)} %get-tuple-element.25), channel_id=1, source_target_pairs={{0,8},{8,16},{16,24},{1,9},{9,17},{17,25},{2,10},{10,18},{18,26},{... | collective-permute-start | bytes 196616 | tf_op jit(solution)/shard_map/ppermute | solution.py:21
  50.5 6.2 %collective-permute-start.7 = (f32[64,2,128]{2,0,1:T(8,128)S(1)}, f32[64,2,128]{2,0,1:T(8,128)S(1)}, u32[]{:S(2)}, u32[]{:S(2)}) collective-permute-start(f32[64,2,128]{2,0,1:T(8,128)S(1)} %get-tuple-element.26), channel_id=1, source_target_pairs={{8,0},{16,8},{24,16},{9,1},{17,9},{25,17},{10,2},{18,10},{26,18},{... | collective-permute-start | bytes 196616 | tf_op jit(solution)/shard_map/ppermute | solution.py:22
  60.7 126.5 %all-gather.5.cloned.1.call-start = ((), (), s32[]{:S(2)}) async-start(), calls=%async_computation.1 | async-start | bytes 12582912 | tf_op jit(solution)/shard_map/all_gather | solution.py:64
  193.6 24.8 %collective-permute-start.8 = (f32[256,1024]{1,0:T(8,128)S(1)}, f32[256,1024]{1,0:T(8,128)S(1)}, u32[]{:S(2)}, u32[]{:S(2)}) collective-permute-start(f32[256,1024]{1,0:T(8,128)S(1)} %fusion.3), channel_id=1, source_target_pairs={{0,8},{8,0},{16,24},{24,16},{1,9},{9,1},{17,25},{25,17},{2,10},{10... | collective-permute-start | bytes 3145736 | tf_op jit(solution)/shard_map/ppermute | solution.py:72
  218.5 47.3 %collective-permute-start.9 = (f32[256,1024]{1,0:T(8,128)S(1)}, f32[256,1024]{1,0:T(8,128)S(1)}, u32[]{:S(2)}, u32[]{:S(2)}) collective-permute-start(f32[256,1024]{1,0:T(8,128)S(1)} %add.330), channel_id=1, source_target_pairs={{0,16},{8,24},{16,0},{24,8},{1,17},{9,25},{17,1},{25,9},{2,18},{10... | collective-permute-start | bytes 3145736 | tf_op jit(solution)/shard_map/ppermute | solution.py:72
Sparse Core Ops, SparseCore 0:
  60.8 20.7 all-gather.2
  83.2 103.9 all-gather.4
